TPU v7x, 32 devices: a whole 2x2x4 slice. The times are simulated.
32 devices in a mesh: dp: 2 (over x), row: 4 (over z), col: 4 (over y, core).
Axes of the slice: x: 2, y: 2, z: 4, core: 2. Of those that a mesh axis runs over, the one named last changes fastest.
Arguments:
- block_in: float32 [2048, 1152], P(('dp', 'col'), 'row'), may hold values from -6 to 6
- labels: int32 [2], P('dp'), may hold values from 0 to 1000
- steps_t: int32 [2], P('dp'), may hold values from 0 to 999
- out_cot: float32 [2048, 1152], P(('dp', 'col'), 'row'), may hold values from -6 to 6
- class_table: float32 [1001, 1152], P(None, 'col'), may hold values from -6 to 6
- w_ada: float32 [1152, 6, 1152], P('col', None, 'row'), may hold values from -0.1875 to 0.1875
- b_ada: float32 [6, 1152], P(None, 'row'), may hold values from -3 to 3
- w_qkv: float32 [1152, 3, 1152], P('row', None, 'col'), may hold values from -0.125 to 0.125
- b_qv: float32 [2, 1152], P(None, 'col'), may hold values from -3 to 3
- w_out: float32 [1152, 1152], P('col', 'row'), may hold values from -3.5 to 3.5
- b_out: float32 [1152], P('row'), may hold values from -3 to 3
- w_up: float32 [1152, 4608], P('row', 'col'), may hold values from -0.1875 to 0.1875
- b_up: float32 [4608], P('col'), may hold values from -3 to 3
- w_down: float32 [4608, 1152], P('col', 'row'), may hold values from -0.09375 to 0.09375
- b_down: float32 [1152], P('row'), may hold values from -3 to 3
Outputs:
- block_out: float32 [2048, 1152], P(('dp', 'col'), 'row')
- in_grad: float32 [2048, 1152], P(('dp', 'col'), 'row')
- table_grad: float32 [1001, 1152], P(None, 'col')
- ada_grad: float32 [1152, 6, 1152], P('col', None, 'row')
- ada_bias_grad: float32 [6, 1152], P(None, 'row')
- qkv_grad: float32 [1152, 3, 1152], P('row', None, 'col')
- qv_bias_grad: float32 [2, 1152], P(None, 'col')
- out_grad: float32 [1152, 1152], P('col', 'row')
- out_bias_grad: float32 [1152], P('row')
- up_grad: float32 [1152, 4608], P('row', 'col')
- up_bias_grad: float32 [4608], P('col')
- down_grad: float32 [4608, 1152], P('col', 'row')
- down_bias_grad: float32 [1152], P('row')
All inputs are finite; a program needn't handle non-finite values.
Results may differ from a plain program's by a relative error of at most 0.0003.
Values sent between devices are 32-bit elements; how exact they have to be, the bound alone decides.
No kernel may reach another device: no remote copies, remote signals or barrier semaphores. Data moves between devices by JAX's collectives and lax.ppermute only.
A program may use at most 128 MiB of HBM per device.

v0:
```python
from functools import partial
import math
import jax
import jax.numpy as jnp
from jax import lax
from jax.sharding import PartitionSpec as P

D = 1152
HD = 72
SEQ = 1024
exact_mode = lax.Precision.HIGHEST
norm_epsilon = 1e-06


def matmul(left, right):
    return jnp.dot(left, right, precision=exact_mode, preferred_element_type=jnp.float32)


def inner_rows(left, right):
    return lax.dot_general(
        left,
        right,
        (((0,), (0,)), ((), ())),
        precision=exact_mode,
        preferred_element_type=jnp.float32,
    )


def gather_col(local):
    return lax.all_gather(local, "col", axis=0, tiled=True)


def gather_row(local):
    return lax.all_gather(local, "row", axis=0, tiled=True)


def gather_keys(local):
    return lax.all_gather(local, "row", axis=0, tiled=True)


def project_up(local, matrix):
    gathered = gather_col(local)
    own_rows = gathered.shape[0] // lax.axis_size("row")

    def partial_term(start, row_count):
        return matmul(gathered, matrix)

    return (
        gathered,
        lax.psum_scatter(
            partial_term(jnp.int32(0), own_rows * lax.axis_size("row")),
            "row",
            scatter_dimension=0,
            tiled=True,
        ),
    )


def project_down(local, matrix):
    gathered = gather_row(local)
    own_rows = gathered.shape[0] // lax.axis_size("col")

    def partial_term(start, row_count):
        return matmul(lax.dynamic_slice_in_dim(gathered, start, row_count, 0), matrix)

    return (
        gathered,
        lax.psum_scatter(
            partial_term(jnp.int32(0), own_rows * lax.axis_size("col")),
            "col",
            scatter_dimension=0,
            tiled=True,
        ),
    )


def width_total(values):
    return lax.psum(jnp.sum(values, axis=1, keepdims=True), "row")


def width_pair(first, second):
    return lax.psum(
        (jnp.sum(first, axis=1, keepdims=True), jnp.sum(second, axis=1, keepdims=True)), "row"
    )


def normalize(values):
    center = width_total(values) / D
    centred = values - center
    spread = width_total(centred * centred) / D
    inverse = lax.rsqrt(spread + norm_epsilon)
    return (centred * inverse, inverse)


def normalize_back(grad_values, normed, inverse):
    totals, along = width_pair(grad_values, grad_values * normed)
    return inverse * (grad_values - totals / D - normed * (along / D))


def attend(queries, keyvals):
    query_rows, head_count, head_dim = queries.shape
    block_rows = min(query_rows, 512)
    factor = 1.0 / math.sqrt(head_dim)

    def attend_block(index):
        scores = jnp.einsum("qhd,khd->hqk", queries, keyvals[:, 0], precision=exact_mode) * factor
        weights = jnp.exp(scores)
        row_sums = jnp.sum(weights, axis=2, keepdims=True)
        result = jnp.einsum("hqk,khd->qhd", weights / row_sums, keyvals[:, 1], precision=exact_mode)
        return (result, jnp.log(row_sums[:, :, 0]))

    results, log_sums = lax.map(attend_block, jnp.arange(query_rows // block_rows))
    return (results.reshape(query_rows, head_count, head_dim), log_sums)


def attend_back(queries, keyvals, attended, log_sums, d_attended):
    query_rows, head_count, head_dim = queries.shape
    block_rows = min(query_rows, 512)
    factor = 1.0 / math.sqrt(head_dim)

    def back_block(kv_totals, scan_item):
        index, block_logs = scan_item
        scores = jnp.einsum("qhd,khd->hqk", queries, keyvals[:, 0], precision=exact_mode) * factor
        weights = jnp.exp(scores - block_logs[:, :, None])
        d_weights = jnp.einsum("qhd,khd->hqk", d_attended, keyvals[:, 1], precision=exact_mode)
        row_dots = jnp.transpose(jnp.sum(d_attended * attended, axis=2))
        d_scores = weights * (d_weights - row_dots[:, :, None]) * factor
        d_query = jnp.einsum("hqk,khd->qhd", d_scores, keyvals[:, 0], precision=exact_mode)
        d_key = jnp.einsum("hqk,qhd->khd", d_scores, queries, precision=exact_mode)
        d_value = jnp.einsum("hqk,qhd->khd", weights, d_attended, precision=exact_mode)
        current = kv_totals
        kv_totals = current + jnp.stack([d_key, d_value], axis=1)
        return (kv_totals, d_query)

    kv_grads, d_queries = lax.scan(
        back_block, jnp.zeros_like(keyvals), (jnp.arange(query_rows // block_rows), log_sums)
    )
    return (d_queries.reshape(query_rows, head_count, head_dim), kv_grads)


def shards(
    block_in,
    labels,
    steps_t,
    out_cot,
    class_table,
    w_ada,
    b_ada,
    w_qkv,
    b_qv,
    w_out,
    b_out,
    w_up,
    b_up,
    w_down,
    b_down,
):
    tok_local, width_row = block_in.shape
    width_col = w_out.shape[0]
    latent_count = labels.shape[0]
    head_local = width_col // HD
    label_hot = (labels[:, None] == jnp.arange(class_table.shape[0])[None, :]).astype(jnp.float32)
    feature = lax.axis_index("col") * width_col + jnp.arange(width_col)
    half_width = D // 2
    frequency = jnp.exp(
        -math.log(10000.0) * (feature % half_width).astype(jnp.float32) / half_width
    )
    angles = steps_t.astype(jnp.float32)[:, None] * frequency[None, :]
    condition = matmul(label_hot, class_table) + jnp.where(
        feature[None, :] < half_width, jnp.cos(angles), jnp.sin(angles)
    )
    silu_cond, silu_pull = jax.vjp(jax.nn.silu, condition)
    ada_terms = jnp.einsum("lc,cjr->ljr", silu_cond, w_ada, precision=exact_mode)
    modulation = lax.psum(ada_terms, "col") + b_ada
    token_index = lax.axis_index("col") * tok_local + jnp.arange(tok_local)
    member = (token_index[:, None] // SEQ == jnp.arange(latent_count)[None, :]).astype(jnp.float32)
    per_token = matmul(member, modulation.reshape(latent_count, 6 * width_row)).reshape(
        tok_local, 6, width_row
    )
    shift_one = per_token[:, 0]
    scale_one = per_token[:, 1]
    gate_one = per_token[:, 2]
    shift_two = per_token[:, 3]
    scale_two = per_token[:, 4]
    gate_two = per_token[:, 5]
    normed_one, inverse_one = normalize(block_in)
    hidden_one = normed_one * (1.0 + scale_one) + shift_one
    qkv_matrix = w_qkv.reshape(width_row, 3 * width_col)
    hidden_one_seen, qkv_local = project_up(hidden_one, qkv_matrix)
    query_rows = qkv_local.shape[0]
    qkv_local = qkv_local.reshape(query_rows, 3, width_col)
    queries = (qkv_local[:, 0] + b_qv[0]).reshape(query_rows, head_local, HD)
    keyval_local = jnp.stack([qkv_local[:, 1], qkv_local[:, 2] + b_qv[1]], axis=1)
    keyval_seen = gather_keys(keyval_local).reshape(-1, 2, head_local, HD)
    attended, log_sums = attend(queries, keyval_seen)
    attended_flat = attended.reshape(query_rows, width_col)
    attended_seen, proj_local = project_down(attended_flat, w_out)
    attn_out = proj_local + b_out
    mixed = block_in + gate_one * attn_out
    normed_two, inverse_two = normalize(mixed)
    hidden_two = normed_two * (1.0 + scale_two) + shift_two
    hidden_two_seen, up_local = project_up(hidden_two, w_up)
    activated, gelu_pull = jax.vjp(partial(jax.nn.gelu, approximate=True), up_local + b_up)
    activated_seen, down_local = project_down(activated, w_down)
    mlp_out = down_local + b_down
    block_out = mixed + gate_two * mlp_out
    hidden_one_all = gather_col(hidden_one)
    keyval_all = gather_keys(keyval_local).reshape(-1, 2, head_local, HD)
    attended_all = gather_row(attended_flat)
    hidden_two_all = gather_col(hidden_two)
    activated_all = gather_row(activated)
    d_mlp = out_cot * gate_two
    d_mlp_all, d_activated = project_up(d_mlp, w_down.T)
    (d_up,) = gelu_pull(d_activated)
    down_grad = inner_rows(activated_all, d_mlp_all)
    down_bias_grad = jnp.sum(d_mlp_all, axis=0)
    d_up_all, d_hidden_two = project_down(d_up, w_up.T)
    up_grad = inner_rows(hidden_two_all, d_up_all)
    up_bias_grad = jnp.sum(d_up_all, axis=0)
    d_mixed = out_cot + normalize_back(d_hidden_two * (1.0 + scale_two), normed_two, inverse_two)
    d_attn = d_mixed * gate_one
    d_attn_all, d_attended = project_up(d_attn, w_out.T)
    out_grad = inner_rows(attended_all, d_attn_all)
    out_bias_grad = jnp.sum(d_attn_all, axis=0)
    d_queries, kv_grads = attend_back(
        queries, keyval_all, attended, log_sums, d_attended.reshape(query_rows, head_local, HD)
    )
    kv_local_grad = lax.psum_scatter(
        kv_grads.reshape(-1, 2, width_col), "row", scatter_dimension=0, tiled=True
    )
    d_qkv = jnp.stack(
        [d_queries.reshape(query_rows, width_col), kv_local_grad[:, 0], kv_local_grad[:, 1]], axis=1
    ).reshape(query_rows, 3 * width_col)
    d_qkv_all, d_hidden_one = project_down(d_qkv, qkv_matrix.T)
    qkv_grad = inner_rows(hidden_one_all, d_qkv_all).reshape(width_row, 3, width_col)
    qv_bias_grad = jnp.stack(
        [jnp.sum(d_qkv_all[:, :width_col], axis=0), jnp.sum(d_qkv_all[:, 2 * width_col :], axis=0)]
    )
    in_grad = d_mixed + normalize_back(d_hidden_one * (1.0 + scale_one), normed_one, inverse_one)
    mod_terms = jnp.stack(
        [
            d_hidden_one,
            d_hidden_one * normed_one,
            d_mixed * attn_out,
            d_hidden_two,
            d_hidden_two * normed_two,
            out_cot * mlp_out,
        ],
        axis=1,
    )
    latent_terms = inner_rows(member, mod_terms.reshape(tok_local, 6 * width_row)).reshape(
        latent_count, 6, width_row
    )
    mod_grads = lax.psum(latent_terms, "col")
    ada_grad = jnp.einsum("lc,ljr->cjr", silu_cond, mod_grads, precision=exact_mode)
    ada_bias_grad = jnp.sum(mod_grads, axis=0)
    silu_grads = lax.psum(jnp.einsum("ljr,cjr->lc", mod_grads, w_ada, precision=exact_mode), "row")
    (cond_grad,) = silu_pull(silu_grads)
    table_grad = inner_rows(label_hot, cond_grad)
    summed = lax.psum(
        (
            table_grad,
            ada_grad,
            ada_bias_grad,
            qkv_grad,
            qv_bias_grad,
            out_grad,
            out_bias_grad,
            up_grad,
            up_bias_grad,
            down_grad,
            down_bias_grad,
        ),
        "dp",
    )
    return (
        block_out,
        in_grad,
        summed[0],
        summed[1],
        summed[2],
        summed[3],
        summed[4],
        summed[5],
        summed[6],
        summed[7],
        summed[8],
        summed[9],
        summed[10],
    )


def solution(mesh):
    in_specs = (
        P(("dp", "col"), "row"),
        P("dp"),
        P("dp"),
        P(("dp", "col"), "row"),
        P(None, "col"),
        P("col", None, "row"),
        P(None, "row"),
        P("row", None, "col"),
        P(None, "col"),
        P("col", "row"),
        P("row"),
        P("row", "col"),
        P("col"),
        P("col", "row"),
        P("row"),
    )
    out_specs = (
        P(("dp", "col"), "row"),
        P(("dp", "col"), "row"),
        P(None, "col"),
        P("col", None, "row"),
        P(None, "row"),
        P("row", None, "col"),
        P(None, "col"),
        P("col", "row"),
        P("row"),
        P("row", "col"),
        P("col"),
        P("col", "row"),
        P("row"),
    )
    return jax.shard_map(shards, mesh=mesh, in_specs=in_specs, out_specs=out_specs, check_vma=False)
```

profile of v0, /device:TPU:0, one launch (start us, length us, event | category | flops | bytes accessed | tf_op | source)
XLA Modules:
  0.0 1210.4 jit_solution(3974382097439372623)
XLA Ops:
  9.7 13.5 %psum.155 = f32[256,1]{0,1:T(1,128)S(1)} all-reduce(f32[256,1]{0,1:T(1,128)S(1)} %bitcast.212), channel_id=1, replica_groups=mesh['dp'=2,'row'=4,'col'=4] {'row'}, use_global_device_ids=true, to_apply=%region_2.3 | all-reduce | flops 256 | bytes 2048 | tf_op jit(solution)/shard_map/psum | solution.py:78
  37.3 10.3 psum.154
  52.8 14.3 %all-gather.10.cloned.1.call-done = f32[1024,288]{0,1:T(8,128)} async-done(((f32[256,288]{0,1:T(8,128)}), f32[1024,288]{0,1:T(8,128)}) %all-gather.10.cloned.1.call-update) | async-done | bytes 1179664 | tf_op jit(solution)/shard_map/all_gather | solution.py:30
  67.1 8.7 fusion.55
  76.5 66.0 %reduce-scatter.10.cloned.1.call-done = f32[256,864]{0,1:T(8,128)} async-done(((f32[1024,864]{0,1:T(8,128)}), f32[256,864]{0,1:T(8,128)}) %reduce-scatter.10.cloned.1.call-update) | async-done | bytes 884752 | tf_op jit(solution)/shard_map/reduce_scatter | solution.py:50
  145.0 50.0 %all-gather.12.cloned.1.call-done = f32[1024,2,288]{0,2,1:T(8,128)} async-done(((f32[256,2,288]{0,2,1:T(8,128)}), f32[1024,2,288]{0,2,1:T(8,128)}) %all-gather.12.cloned.1.call-update) | async-done | bytes 2359312 | tf_op jit(solution)/shard_map/all_gather | solution.py:38
  206.0 29.1 %all-gather.14.cloned.1.call-done = f32[1024,288]{0,1:T(8,128)} async-done(((f32[256,288]{0,1:T(8,128)}), f32[1024,288]{0,1:T(8,128)}) %all-gather.14.cloned.1.call-update) | async-done | bytes 1179664 | tf_op jit(solution)/shard_map/all_gather | solution.py:34
  239.6 24.9 %reduce-scatter.12.cloned.1.call-done = f32[256,288]{0,1:T(8,128)} async-done(((f32[1024,288]{0,1:T(8,128)}), f32[256,288]{0,1:T(8,128)}) %reduce-scatter.12.cloned.1.call-update) | async-done | bytes 294928 | tf_op jit(solution)/shard_map/reduce_scatter | solution.py:68
  265.7 11.7 psum.157
  277.4 8.9 psum.158
  290.1 15.3 %all-gather.16.cloned.1.call-done = f32[1024,288]{0,1:T(8,128)} async-done(((f32[256,288]{0,1:T(8,128)}), f32[1024,288]{0,1:T(8,128)}) %all-gather.16.cloned.1.call-update) | async-done | bytes 1179664 | tf_op jit(solution)/shard_map/all_gather | solution.py:30
  305.4 11.1 fusion.57
  325.0 11.2 fusion.59
  336.2 76.4 %reduce-scatter.14.cloned.1.call-done = f32[256,1152]{1,0:T(8,128)} async-done(((f32[1024,1152]{1,0:T(8,128)}), f32[256,1152]{1,0:T(8,128)}) %reduce-scatter.14.cloned.1.call-update) | async-done | bytes 1179664 | tf_op jit(solution)/shard_map/reduce_scatter | solution.py:50
  412.6 88.2 %reduce-scatter.18.cloned.1.call-done = f32[256,1152]{1,0:T(8,128)} async-done(((f32[1024,1152]{1,0:T(8,128)}), f32[256,1152]{1,0:T(8,128)}) %reduce-scatter.18.cloned.1.call-update) | async-done | bytes 1179664 | tf_op jit(solution)/shard_map/reduce_scatter | solution.py:50
  505.8 88.9 %all-gather.22.cloned.1.call-done = f32[1024,1152]{1,0:T(8,128)} async-done(((f32[256,1152]{1,0:T(8,128)}), f32[1024,1152]{1,0:T(8,128)}) %all-gather.22.cloned.1.call-update) | async-done | bytes 4718608 | tf_op jit(solution)/shard_map/all_gather | solution.py:34
  594.7 8.8 fusion.60
  603.6 81.1 %all-gather.18.cloned.1.call-done = f32[1024,1152]{1,0:T(8,128)} async-done(((f32[256,1152]{1,0:T(8,128)}), f32[1024,1152]{1,0:T(8,128)}) %all-gather.18.cloned.1.call-update) | async-done | bytes 4718608 | tf_op jit(solution)/shard_map/all_gather | solution.py:34
  684.7 8.8 fusion.58
  693.6 18.2 %reduce-scatter.20.cloned.1.call-done = f32[256,288]{0,1:T(8,128)} async-done(((f32[1024,288]{0,1:T(8,128)}), f32[256,288]{0,1:T(8,128)}) %reduce-scatter.20.cloned.1.call-update) | async-done | bytes 294928 | tf_op jit(solution)/shard_map/reduce_scatter | solution.py:68
  713.4 12.4 %all-reduce.1 = (f32[256,1]{0,1:T(1,128)}, f32[256,1]{0,1:T(1,128)}) all-reduce(f32[256,1]{0,1:T(1,128)} %bitcast.211, f32[256,1]{0,1:T(1,128)} %bitcast.210), channel_id=1, replica_groups=mesh['dp'=2,'row'=4,'col'=4] {'row'}, use_global_device_ids=true, to_apply=%region_19.20 | all-reduce | flops 512 | bytes 4096 | tf_op jit(solution)/shard_map/psum | solution.py:82
  727.1 13.4 %reduce-scatter.16.cloned.1.call-done = f32[256,288]{0,1:T(8,128)} async-done(((f32[1024,288]{0,1:T(8,128)}), f32[256,288]{0,1:T(8,128)}) %reduce-scatter.16.cloned.1.call-update) | async-done | bytes 294928 | tf_op jit(solution)/shard_map/reduce_scatter | solution.py:68
  743.2 17.3 %all-gather.24.cloned.1.call-done = f32[1024,288]{0,1:T(8,128)} async-done(((f32[256,288]{0,1:T(8,128)}), f32[1024,288]{0,1:T(8,128)}) %all-gather.24.cloned.1.call-update) | async-done | bytes 1179664 | tf_op jit(solution)/shard_map/all_gather | solution.py:30
  765.7 28.7 %reduce-scatter.22.cloned.1.call-done = f32[256,288]{0,1:T(8,128)} async-done(((f32[1024,288]{0,1:T(8,128)}), f32[256,288]{0,1:T(8,128)}) %reduce-scatter.22.cloned.1.call-update) | async-done | bytes 294928 | tf_op jit(solution)/shard_map/reduce_scatter | solution.py:50
  818.1 39.6 %reduce-scatter.24.cloned.1.call-done = f32[256,2,288]{0,2,1:T(8,128)} async-done(((f32[1024,2,288]{0,2,1:T(8,128)}), f32[256,2,288]{0,2,1:T(8,128)}) %reduce-scatter.24.cloned.1.call-update) | async-done | bytes 589840 | tf_op jit(solution)/shard_map/reduce_scatter | solution.py:228
  859.9 69.3 %all-gather.26.cloned.1.call-done = f32[1024,864]{0,1:T(8,128)} async-done(((f32[256,864]{0,1:T(8,128)}), f32[1024,864]{0,1:T(8,128)}) %all-gather.26.cloned.1.call-update) | async-done | bytes 3538960 | tf_op jit(solution)/shard_map/all_gather | solution.py:34
  938.4 9.1 fusion.66
  947.5 8.5 fusion.65
  970.1 10.5 psum.163
  985.7 10.3 all-reduce
  1007.8 10.3 all-reduce.2
  1021.3 170.0 %all-reduce.6.cloned.1.call-done = (f32[1001,288]{0,1:T(8,128)}, f32[288,6,288]{2,0,1:T(8,128)}, f32[288,3,288]{0,2,1:T(8,128)}, f32[288,288]{1,0:T(8,128)}, f32[288,1152]{1,0:T(8,128)}, /*index=5*/f32[1152,288]{0,1:T(8,128)}) async-done(((f32[1001,288]{0,1:T(8,128)}, f32[288,6,288]{2,0,1:T(8,128)}, f32[288,3,288]{0,2,1:T(8,128)}, f32[288,288]{1,0:T(8,128)}, f32[288,1152]{1,0:T(8,128)}, ...) | async-done | bytes 7125136 | tf_op jit(solution)/shard_map/psum | solution.py:260
  (214 shorter events, 149.6 us)
Async XLA Ops:
  7.2 28.7 %copy-start = (f32[288,6,288]{2,0,1:T(8,128)S(1)}, f32[288,6,288]{2,0,1:T(8,128)}, u32[]{:S(2)}) copy-start(f32[288,6,288]{2,0,1:T(8,128)} %param.20) | copy-start | bytes 5971972
  7.2 59.9 %all-gather.10.cloned.1.call-start = ((), (), s32[]{:S(2)}) async-start(), calls=%async_computation.9 | async-start | bytes 1474560 | tf_op jit(solution)/shard_map/all_gather | solution.py:30
  32.6 15.2 %copy-start.28 = (f32[256,1]{0,1:T(1,128)}, f32[256,1]{0,1:T(1,128)S(1)}, u32[]{:S(2)}) copy-start(f32[256,1]{0,1:T(1,128)S(1)} %add_rsqrt_fusion.1) | copy-start | bytes 3076
  49.8 92.6 %reduce-scatter.10.cloned.1.call-start = ((), (), s32[]{:S(2)}) async-start(), calls=%async_computation.10 | async-start | bytes 4423680 | tf_op jit(solution)/shard_map/reduce_scatter | solution.py:50
  75.8 119.2 %all-gather.12.cloned.1.call-start = ((), (), s32[]{:S(2)}) async-start(), calls=%async_computation.11 | async-start | bytes 2949120 | tf_op jit(solution)/shard_map/all_gather | solution.py:38
  143.7 56.9 %copy-start.17 = (f32[256,1,288]{0,2,1:T(8,128)}, f32[256,1,288]{0,2,1:T(8,128)S(1)}, u32[]{:S(2)}) copy-start(f32[256,1,288]{0,2,1:T(8,128)S(1)} %get-tuple-element.100) | copy-start | bytes 884740
  144.6 90.5 %all-gather.14.cloned.1.call-start = ((), (), s32[]{:S(2)}) async-start(), calls=%async_computation.12 | async-start | bytes 1474560 | tf_op jit(solution)/shard_map/all_gather | solution.py:34
  145.0 55.7 %copy-start.31 = (f32[4,72]{1,0:T(4,128)}, f32[4,72]{1,0:T(4,128)S(1)}, u32[]{:S(2)}) copy-start(f32[4,72]{1,0:T(4,128)S(1)} %add.211) | copy-start | bytes 3460
  200.7 34.4 %copy-start.21 = (f32[288,288]{1,0:T(8,128)S(1)}, f32[288,288]{1,0:T(8,128)}, u32[]{:S(2)}) copy-start(f32[288,288]{1,0:T(8,128)} %param.24) | copy-start | bytes 995332
  205.9 58.6 %copy-start.40 = (f32[288]{0:T(512)S(1)}, f32[288]{0:T(512)}, u32[]{:S(2)}) copy-start(f32[288]{0:T(512)} %param.25) | copy-start | bytes 3460
  205.9 58.6 %reduce-scatter.12.cloned.1.call-start = ((), (), s32[]{:S(2)}) async-start(), calls=%async_computation.13 | async-start | bytes 1474560 | tf_op jit(solution)/shard_map/reduce_scatter | solution.py:68
  239.5 47.6 %copy-start.14 = (f32[256,288]{0,1:T(8,128)S(1)}, f32[256,288]{0,1:T(8,128)}, u32[]{:S(2)}) copy-start(f32[256,288]{0,1:T(8,128)} %param.18) | copy-start | bytes 884740
  239.5 65.9 %all-gather.16.cloned.1.call-start = ((), (), s32[]{:S(2)}) async-start(), calls=%async_computation.14 | async-start | bytes 1474560 | tf_op jit(solution)/shard_map/all_gather | solution.py:30
  289.1 35.9 %all-gather.20.cloned.1.call-start = ((), (), s32[]{:S(2)}) async-start(), calls=%async_computation.18 | async-start | bytes 1474560 | tf_op jit(solution)/shard_map/all_gather | solution.py:30
  289.9 122.7 %reduce-scatter.14.cloned.1.call-start = ((), (), s32[]{:S(2)}) async-start(), calls=%async_computation.15 | async-start | bytes 5898240 | tf_op jit(solution)/shard_map/reduce_scatter | solution.py:50
  316.5 184.2 %reduce-scatter.18.cloned.1.call-start = ((), (), s32[]{:S(2)}) async-start(), calls=%async_computation.19 | async-start | bytes 5898240 | tf_op jit(solution)/shard_map/reduce_scatter | solution.py:50
  336.2 258.5 %all-gather.22.cloned.1.call-start = ((), (), s32[]{:S(2)}) async-start(), calls=%async_computation.20 | async-start | bytes 5898240 | tf_op jit(solution)/shard_map/all_gather | solution.py:34
  504.7 180.0 %all-gather.18.cloned.1.call-start = ((), (), s32[]{:S(2)}) async-start(), calls=%async_computation.16 | async-start | bytes 5898240 | tf_op jit(solution)/shard_map/all_gather | solution.py:34
  505.4 206.4 %reduce-scatter.20.cloned.1.call-start = ((), (), s32[]{:S(2)}) async-start(), calls=%async_computation.21 | async-start | bytes 1474560 | tf_op jit(solution)/shard_map/reduce_scatter | solution.py:68
  603.5 137.0 %reduce-scatter.16.cloned.1.call-start = ((), (), s32[]{:S(2)}) async-start(), calls=%async_computation.17 | async-start | bytes 1474560 | tf_op jit(solution)/shard_map/reduce_scatter | solution.py:68
  693.5 47.0 %copy-start.42 = (f32[288]{0:T(512)S(1)}, f32[288]{0:T(512)}, u32[]{:S(2)}) copy-start(f32[288]{0:T(512)} %param.29) | copy-start | bytes 3460
  693.5 67.0 %all-gather.24.cloned.1.call-start = ((), (), s32[]{:S(2)}) async-start(), calls=%async_computation.22 | async-start | bytes 1474560 | tf_op jit(solution)/shard_map/all_gather | solution.py:30
  742.9 51.5 %copy-start.26 = (f32[4,72,256]{2,1,0:T(8,128)S(1)}, f32[4,72,256]{2,1,0:T(8,128)}, u32[]{:S(2)}) copy-start(f32[4,72,256]{2,1,0:T(8,128)} %fusion) | copy-start | bytes 884740
  742.9 51.5 %reduce-scatter.22.cloned.1.call-start = ((), (), s32[]{:S(2)}) async-start(), calls=%async_computation.23 | async-start | bytes 1474560 | tf_op jit(solution)/shard_map/reduce_scatter | solution.py:50
  765.0 92.8 %reduce-scatter.24.cloned.1.call-start = ((), (), s32[]{:S(2)}) async-start(), calls=%async_computation.24 | async-start | bytes 2949120 | tf_op jit(solution)/shard_map/reduce_scatter | solution.py:228
  811.2 118.0 %all-gather.26.cloned.1.call-start = ((), (), s32[]{:S(2)}) async-start(), calls=%async_computation.25 | async-start | bytes 4423680 | tf_op jit(solution)/shard_map/all_gather | solution.py:34
  859.8 106.0 %reduce-scatter.26.cloned.1.call-start = ((), (), s32[]{:S(2)}) async-start(), calls=%async_computation.26 | async-start | bytes 1474560 | tf_op jit(solution)/shard_map/reduce_scatter | solution.py:68
  936.7 254.5 %all-reduce.6.cloned.1.call-start = ((), (), s32[]{:S(2)}) async-start(), calls=%async_computation.27 | async-start | bytes 16515072 | tf_op jit(solution)/shard_map/psum | solution.py:260
  982.4 13.6 %copy-start.36 = (f32[288]{0:T(512)S(1)}, f32[288]{0:T(512)}, u32[]{:S(2)}) copy-start(f32[288]{0:T(512)} %copy-done.35) | copy-start | bytes 3460
  982.4 13.6 %copy-start.44 = (f32[288]{0:T(512)S(1)}, f32[288]{0:T(512)}, u32[]{:S(2)}) copy-start(f32[288]{0:T(512)} %get-tuple-element.89) | copy-start | bytes 3460
  982.4 13.6 %copy-start.37 = (f32[1,1001]{1,0:T(1,128)S(1)}, f32[1,1001]{1,0:T(1,128)}, u32[]{:S(2)}) copy-start(f32[1,1001]{1,0:T(1,128)} %compare_convert_fusion) | copy-start | bytes 12016
  1005.3 14.1 %copy-start.20 = (f32[256,288]{0,1:T(8,128)S(1)}, f32[256,288]{0,1:T(8,128)}, u32[]{:S(2)}) copy-start(f32[256,288]{0,1:T(8,128)} %get-tuple-element.92) | copy-start | bytes 884740
  (35 other events, 171.1 us)
Sparse Core Ops, SparseCore 0:
  49.9 17.1 all-gather.9
  75.9 66.4 reduce-scatter.9
  144.8 50.1 all-gather.11
  206.0 29.0 all-gather.13
  239.6 24.8 reduce-scatter.11
  289.2 16.1 all-gather.15
  307.5 17.4 all-gather.19
  327.3 85.2 reduce-scatter.13
  414.9 85.7 reduce-scatter.17
  504.8 89.8 all-gather.21
  596.9 87.7 all-gather.17
  687.7 24.0 reduce-scatter.19
  714.9 25.5 reduce-scatter.15
  743.0 17.4 all-gather.23
  765.1 29.3 reduce-scatter.21
  811.4 46.3 reduce-scatter.23
  859.9 69.2 all-gather.25
  936.8 24.1 reduce-scatter.25
  997.4 193.8 all-reduce.5
where the time goes:
time: 1220 us; the launch traced here: 1210 us
  waiting for transfers between devices  901 us (74%)
  matrix products  130 us (11%)
  blocking collectives  96.1 us (8%)
  other arithmetic  44 us (4%)
  local copies, waits for them, and re-layouts  20.7 us (2%)
  between operations  16.1 us (1%)
    all_gather x4, waiting for transfers between devices, gather_row(): return lax.all_gather(local, 'row', axis=0, tiled=True)  268 us
    reduce_scatter x4, waiting for transfers between devices, project_up(): lax.psum_scatter(partial_term(jnp.int32(0), own_rows * lax.axis_size('row...  259 us
    psum x1, waiting for transfers between devices, shards(): lax.psum((table_grad, ada_grad, ada_bias_grad, qkv_grad, qv_bias_grad, ou...  170 us
    dot_general x9, matrix products, matmul(): jnp.dot(left, right, precision=exact_mode, preferred_element_type=jnp.flo...  66.8 us
    reduce_scatter x4, waiting for transfers between devices, project_down(): lax.psum_scatter(partial_term(jnp.int32(0), own_rows * lax.axis_size('col...  56.6 us
    all_gather x4, waiting for transfers between devices, gather_col(): return lax.all_gather(local, 'col', axis=0, tiled=True)  55.3 us
    all_gather x1, waiting for transfers between devices, gather_keys(): return lax.all_gather(local, 'row', axis=0, tiled=True)  50 us
    psum x4, blocking collectives, width_total(): return lax.psum(jnp.sum(values, axis=1, keepdims=True), 'row')  42.4 us
  transfers between devices with their start and end apart: 19, of which 18 were waited for; matrix products, arithmetic and copies ran while one was open for 8% of the time, Pallas kernels for 0%

commit v1 on v0

--- a/solution.py
+++ b/solution.py
@@ -10,6 +10,19 @@
 SEQ = 1024
 exact_mode = lax.Precision.HIGHEST
 norm_epsilon = 1e-06
+
+
+def collect(x, axis, dim):
+    ways = lax.axis_size(axis)
+    up = [(d, (d + 1) % ways) for d in range(ways)]
+    down = [(d, (d - 1) % ways) for d in range(ways)]
+    earlier, later = ([x], [x])
+    for _ in range(ways // 2):
+        earlier.append(lax.ppermute(earlier[-1], axis, up))
+    for _ in range((ways - 1) // 2):
+        later.append(lax.ppermute(later[-1], axis, down))
+    line = jnp.concatenate([*earlier[::-1], *later[1:]], axis=dim)
+    return jnp.roll(line, (lax.axis_index(axis) - ways // 2) * x.shape[dim], axis=dim)
 
 
 def matmul(left, right):
@@ -31,7 +44,7 @@
 
 
 def gather_row(local):
-    return lax.all_gather(local, "row", axis=0, tiled=True)
+    return collect(local, "row", 0)
 
 
 def gather_keys(local):

time: 1220 us -> 1170 us (0.959)
  waiting for transfers between devices: 901 us -> 800 us
  starting transfers between devices: 2.36 us -> 44.3 us
  other arithmetic: 44 us -> 56.6 us
    all_gather x4 -> x0, waiting for transfers between devices: 268 us -> none  [gather_row(): return lax.all_gather(local, 'row', axis=0, tiled=True)]
    ppermute x0 -> x12, waiting for transfers between devices: none -> 182 us  [the longest x8 155 us: collect(): earlier.append(lax.ppermute(earlier[-1], axis, up))]
    ppermute x0 -> x12, starting transfers between devices: none -> 42.4 us  [the longest x8 29.1 us: collect(): earlier.append(lax.ppermute(earlier[-1], axis, up))]
    reduce_scatter x4, waiting for transfers between devices: 56.6 us -> 39.4 us  [project_down(): lax.psum_scatter(partial_term(jnp.int32(0), own_rows * lax.axis_size('col...]
    unnamed x105 -> x118, local copies, waits for them, and re-layouts: 19.3 us -> 28 us
  transfers between devices with their start and end apart: 19 -> 27, of which waited for: 18 -> 26; matrix products, arithmetic and copies ran while one was open for 8% -> 9% of each run, Pallas kernels for 0% -> 0%
where the time goes in v1:
time: 1170 us; the launch traced here: 1160 us
  waiting for transfers between devices  800 us (68%)
  matrix products  121 us (10%)
  blocking collectives  97.7 us (8%)
  other arithmetic  56.6 us (5%)
  starting transfers between devices  44.3 us (4%)
  local copies, waits for them, and re-layouts  28.9 us (2%)
  between operations  16.2 us (1%)
    reduce_scatter x4, waiting for transfers between devices, project_up(): lax.psum_scatter(partial_term(jnp.int32(0), own_rows * lax.axis_size('row...  260 us
    psum x1, waiting for transfers between devices, shards(): lax.psum((table_grad, ada_grad, ada_bias_grad, qkv_grad, qv_bias_grad, ou...  173 us
    ppermute x8, waiting for transfers between devices, collect(): earlier.append(lax.ppermute(earlier[-1], axis, up))  155 us
    dot_general x9, matrix products, matmul(): jnp.dot(left, right, precision=exact_mode, preferred_element_type=jnp.flo...  57.8 us
    all_gather x4, waiting for transfers between devices, gather_col(): return lax.all_gather(local, 'col', axis=0, tiled=True)  55.6 us
    all_gather x1, waiting for transfers between devices, gather_keys(): return lax.all_gather(local, 'row', axis=0, tiled=True)  50 us
    psum x4, blocking collectives, width_total(): return lax.psum(jnp.sum(values, axis=1, keepdims=True), 'row')  42.5 us
    reduce_scatter x4, waiting for transfers between devices, project_down(): lax.psum_scatter(partial_term(jnp.int32(0), own_rows * lax.axis_size('col...  39.4 us
  transfers between devices with their start and end apart: 27, of which 26 were waited for; matrix products, arithmetic and copies ran while one was open for 9% of the time, Pallas kernels for 0%

profile of v1, /device:TPU:0, one launch (start us, length us, event | category | flops | bytes accessed | tf_op | source)
XLA Modules:
  0.0 1164.9 jit_solution(13116228403729882474)
XLA Ops:
  9.7 13.5 %psum.155 = f32[256,1]{0,1:T(1,128)S(1)} all-reduce(f32[256,1]{0,1:T(1,128)S(1)} %bitcast.214), channel_id=1, replica_groups=mesh['dp'=2,'row'=4,'col'=4] {'row'}, use_global_device_ids=true, to_apply=%region_2.3 | all-reduce | flops 256 | bytes 2048 | tf_op jit(solution)/shard_map/psum | solution.py:91
  37.8 10.1 psum.154
  53.3 14.3 %all-gather.6.cloned.1.call-done = f32[1024,288]{0,1:T(8,128)} async-done(((f32[256,288]{0,1:T(8,128)}), f32[1024,288]{0,1:T(8,128)}) %all-gather.6.cloned.1.call-update) | async-done | bytes 1179664 | tf_op jit(solution)/shard_map/all_gather | solution.py:43
  77.0 66.0 %reduce-scatter.10.cloned.1.call-done = f32[256,864]{0,1:T(8,128)} async-done(((f32[1024,864]{0,1:T(8,128)}), f32[256,864]{0,1:T(8,128)}) %reduce-scatter.10.cloned.1.call-update) | async-done | bytes 884752 | tf_op jit(solution)/shard_map/reduce_scatter | solution.py:63
  145.4 50.0 %all-gather.8.cloned.1.call-done = f32[1024,2,288]{0,2,1:T(8,128)} async-done(((f32[256,2,288]{0,2,1:T(8,128)}), f32[1024,2,288]{0,2,1:T(8,128)}) %all-gather.8.cloned.1.call-update) | async-done | bytes 2359312 | tf_op jit(solution)/shard_map/all_gather | solution.py:51
  236.7 23.8 %reduce-scatter.12.cloned.1.call-done = f32[256,288]{0,1:T(8,128)} async-done(((f32[1024,288]{0,1:T(8,128)}), f32[256,288]{0,1:T(8,128)}) %reduce-scatter.12.cloned.1.call-update) | async-done | bytes 294928 | tf_op jit(solution)/shard_map/reduce_scatter | solution.py:81
  262.2 11.8 %psum.157 = f32[256,1]{0,1:T(1,128)S(1)} all-reduce(f32[256,1]{0,1:T(1,128)} %bitcast.219), channel_id=1, replica_groups=mesh['dp'=2,'row'=4,'col'=4] {'row'}, use_global_device_ids=true, to_apply=%region_9.11 | all-reduce | flops 256 | bytes 2048 | tf_op jit(solution)/shard_map/psum | solution.py:91
  274.1 8.9 psum.158
  286.6 15.4 %all-gather.10.cloned.1.call-done = f32[1024,288]{0,1:T(8,128)} async-done(((f32[256,288]{0,1:T(8,128)}), f32[1024,288]{0,1:T(8,128)}) %all-gather.10.cloned.1.call-update) | async-done | bytes 1179664 | tf_op jit(solution)/shard_map/all_gather | solution.py:43
  302.0 11.1 fusion.86
  321.5 11.2 fusion.88
  332.8 76.4 %reduce-scatter.14.cloned.1.call-done = f32[256,1152]{1,0:T(8,128)} async-done(((f32[1024,1152]{1,0:T(8,128)}), f32[256,1152]{1,0:T(8,128)}) %reduce-scatter.14.cloned.1.call-update) | async-done | bytes 1179664 | tf_op jit(solution)/shard_map/reduce_scatter | solution.py:63
  409.1 88.1 %reduce-scatter.18.cloned.1.call-done = f32[256,1152]{1,0:T(8,128)} async-done(((f32[1024,1152]{1,0:T(8,128)}), f32[256,1152]{1,0:T(8,128)}) %reduce-scatter.18.cloned.1.call-update) | async-done | bytes 1179664 | tf_op jit(solution)/shard_map/reduce_scatter | solution.py:63
  506.1 25.4 %collective-permute-done.6 = f32[256,1152]{1,0:T(8,128)S(1)} collective-permute-done((f32[256,1152]{1,0:T(8,128)S(1)}, f32[256,1152]{1,0:T(8,128)S(1)}, u32[]{:S(2)}, u32[]{:S(2)}) %collective-permute-start.6) | collective-permute-done | bytes 1179680 | tf_op jit(solution)/shard_map/ppermute | solution.py:21
  535.3 21.5 %collective-permute-done.3 = f32[256,1152]{1,0:T(8,128)} collective-permute-done((f32[256,1152]{1,0:T(8,128)}, f32[256,1152]{1,0:T(8,128)}, u32[]{:S(2)}, u32[]{:S(2)}) %collective-permute-start.3) | collective-permute-done | bytes 1179680 | tf_op jit(solution)/shard_map/ppermute | solution.py:21
  556.8 24.7 %collective-permute-start.4 = (f32[256,1152]{1,0:T(8,128)}, f32[256,1152]{1,0:T(8,128)}, u32[]{:S(2)}, u32[]{:S(2)}) collective-permute-start(f32[256,1152]{1,0:T(8,128)} %collective-permute-done.3), channel_id=1, source_target_pairs={{0,4},{4,8},{8,12},{12,0},{1,5},{5,9},{9,13},{13,1},{2,6},{6,10},{... | collective-permute-start | bytes 3538952 | tf_op jit(solution)/shard_map/ppermute | solution.py:21
  582.1 25.3 %collective-permute-done.7 = f32[256,1152]{1,0:T(8,128)S(1)} collective-permute-done((f32[256,1152]{1,0:T(8,128)S(1)}, f32[256,1152]{1,0:T(8,128)S(1)}, u32[]{:S(2)}, u32[]{:S(2)}) %collective-permute-start.7) | collective-permute-done | bytes 1179680 | tf_op jit(solution)/shard_map/ppermute | solution.py:21
  623.8 8.7 collective-permute-done.5
  632.5 24.2 %collective-permute-done.4 = f32[256,1152]{1,0:T(8,128)} collective-permute-done((f32[256,1152]{1,0:T(8,128)}, f32[256,1152]{1,0:T(8,128)}, u32[]{:S(2)}, u32[]{:S(2)}) %collective-permute-start.4) | collective-permute-done | bytes 1179680 | tf_op jit(solution)/shard_map/ppermute | solution.py:21
  675.0 12.4 %all-reduce.1 = (f32[256,1]{0,1:T(1,128)}, f32[256,1]{0,1:T(1,128)}) all-reduce(f32[256,1]{0,1:T(1,128)} %bitcast.213, f32[256,1]{0,1:T(1,128)} %bitcast.212), channel_id=1, replica_groups=mesh['dp'=2,'row'=4,'col'=4] {'row'}, use_global_device_ids=true, to_apply=%region_19.22 | all-reduce | flops 512 | bytes 4096 | tf_op jit(solution)/shard_map/psum | solution.py:95
  688.6 13.3 %reduce-scatter.16.cloned.1.call-done = f32[256,288]{0,1:T(8,128)} async-done(((f32[1024,288]{0,1:T(8,128)}), f32[256,288]{0,1:T(8,128)}) %reduce-scatter.16.cloned.1.call-update) | async-done | bytes 294928 | tf_op jit(solution)/shard_map/reduce_scatter | solution.py:81
  704.4 17.5 %all-gather.14.cloned.1.call-done = f32[1024,288]{0,1:T(8,128)} async-done(((f32[256,288]{0,1:T(8,128)}), f32[1024,288]{0,1:T(8,128)}) %all-gather.14.cloned.1.call-update) | async-done | bytes 1179664 | tf_op jit(solution)/shard_map/all_gather | solution.py:43
  726.7 29.2 %reduce-scatter.22.cloned.1.call-done = f32[256,288]{0,1:T(8,128)} async-done(((f32[1024,288]{0,1:T(8,128)}), f32[256,288]{0,1:T(8,128)}) %reduce-scatter.22.cloned.1.call-update) | async-done | bytes 294928 | tf_op jit(solution)/shard_map/reduce_scatter | solution.py:63
  779.8 39.4 %reduce-scatter.24.cloned.1.call-done = f32[256,2,288]{0,2,1:T(8,128)} async-done(((f32[1024,2,288]{0,2,1:T(8,128)}), f32[256,2,288]{0,2,1:T(8,128)}) %reduce-scatter.24.cloned.1.call-update) | async-done | bytes 589840 | tf_op jit(solution)/shard_map/reduce_scatter | solution.py:241
  821.2 22.0 %collective-permute-done.9 = f32[256,864]{0,1:T(8,128)S(1)} collective-permute-done((f32[256,864]{0,1:T(8,128)S(1)}, f32[256,864]{0,1:T(8,128)S(1)}, u32[]{:S(2)}, u32[]{:S(2)}) %collective-permute-start.9) | collective-permute-done | bytes 884768 | tf_op jit(solution)/shard_map/ppermute | solution.py:21
  847.0 20.5 %collective-permute-done.10 = f32[256,864]{0,1:T(8,128)S(1)} collective-permute-done((f32[256,864]{0,1:T(8,128)S(1)}, f32[256,864]{0,1:T(8,128)S(1)}, u32[]{:S(2)}, u32[]{:S(2)}) %collective-permute-start.10) | collective-permute-done | bytes 884768 | tf_op jit(solution)/shard_map/ppermute | solution.py:21
  867.9 14.4 %collective-permute-done.11 = f32[256,864]{0,1:T(8,128)S(1)} collective-permute-done((f32[256,864]{0,1:T(8,128)S(1)}, f32[256,864]{0,1:T(8,128)S(1)}, u32[]{:S(2)}, u32[]{:S(2)}) %collective-permute-start.11) | collective-permute-done | bytes 884768 | tf_op jit(solution)/shard_map/ppermute | solution.py:23
  892.4 8.9 fusion.92
  924.4 10.2 psum.163
  939.7 11.1 all-reduce
  958.8 11.4 all-reduce.2
  973.3 173.0 %all-reduce.6.cloned.1.call-done = (f32[1001,288]{0,1:T(8,128)}, f32[288,6,288]{2,0,1:T(8,128)}, f32[288,3,288]{0,2,1:T(8,128)}, f32[288,288]{1,0:T(8,128)}, f32[288,1152]{1,0:T(8,128)}, /*index=5*/f32[1152,288]{0,1:T(8,128)}) async-done(((f32[1001,288]{0,1:T(8,128)}, f32[288,6,288]{2,0,1:T(8,128)}, f32[288,3,288]{0,2,1:T(8,128)}, f32[288,288]{1,0:T(8,128)}, f32[288,1152]{1,0:T(8,128)}, ...) | async-done | bytes 7125136 | tf_op jit(solution)/shard_map/psum | solution.py:273
  (243 shorter events, 235.0 us)
Async XLA Ops:
  7.2 60.4 %all-gather.6.cloned.1.call-start = ((), (), s32[]{:S(2)}) async-start(), calls=%async_computation.9 | async-start | bytes 1474560 | tf_op jit(solution)/shard_map/all_gather | solution.py:43
  32.6 888.3 %copy-start.31 = (f32[256,1]{0,1:T(1,128)}, f32[256,1]{0,1:T(1,128)S(1)}, u32[]{:S(2)}) copy-start(f32[256,1]{0,1:T(1,128)S(1)} %add_rsqrt_fusion.1) | copy-start | bytes 3076
  50.3 92.6 %reduce-scatter.10.cloned.1.call-start = ((), (), s32[]{:S(2)}) async-start(), calls=%async_computation.10 | async-start | bytes 4423680 | tf_op jit(solution)/shard_map/reduce_scatter | solution.py:63
  76.3 119.2 %all-gather.8.cloned.1.call-start = ((), (), s32[]{:S(2)}) async-start(), calls=%async_computation.11 | async-start | bytes 2949120 | tf_op jit(solution)/shard_map/all_gather | solution.py:51
  144.2 56.9 %copy-start.23 = (f32[256,1,288]{0,2,1:T(8,128)}, f32[256,1,288]{0,2,1:T(8,128)S(1)}, u32[]{:S(2)}) copy-start(f32[256,1,288]{0,2,1:T(8,128)S(1)} %get-tuple-element.104) | copy-start | bytes 884740
  145.1 115.4 %reduce-scatter.12.cloned.1.call-start = ((), (), s32[]{:S(2)}) async-start(), calls=%async_computation.12 | async-start | bytes 1474560 | tf_op jit(solution)/shard_map/reduce_scatter | solution.py:81
  145.4 55.7 %copy-start.33 = (f32[4,72]{1,0:T(4,128)}, f32[4,72]{1,0:T(4,128)S(1)}, u32[]{:S(2)}) copy-start(f32[4,72]{1,0:T(4,128)S(1)} %add.236) | copy-start | bytes 3460
  206.9 12.0 %collective-permute-start = (f32[256,288]{0,1:T(8,128)}, f32[256,288]{0,1:T(8,128)}, u32[]{:S(2)}, u32[]{:S(2)}) collective-permute-start(f32[256,288]{0,1:T(8,128)} %bitcast.19), channel_id=1, source_target_pairs={{0,4},{4,8},{8,12},{12,0},{1,5},{5,9},{9,13},{13,1},{2,6},{6,10},{... | collective-permute-start | bytes 884744 | tf_op jit(solution)/shard_map/ppermute | solution.py:21
  206.9 15.3 %collective-permute-start.2 = (f32[256,288]{0,1:T(8,128)}, f32[256,288]{0,1:T(8,128)}, u32[]{:S(2)}, u32[]{:S(2)}) collective-permute-start(f32[256,288]{0,1:T(8,128)} %bitcast.19), channel_id=1, source_target_pairs={{0,12},{4,0},{8,4},{12,8},{1,13},{5,1},{9,5},{13,9},{2,14},{6,2},{... | collective-permute-start | bytes 884744 | tf_op jit(solution)/shard_map/ppermute | solution.py:23
  218.9 11.4 collective-permute-start.1
  236.6 47.1 %copy-start.20 = (f32[256,288]{0,1:T(8,128)S(1)}, f32[256,288]{0,1:T(8,128)}, u32[]{:S(2)}) copy-start(f32[256,288]{0,1:T(8,128)} %param.22) | copy-start | bytes 884740
  236.6 65.4 %all-gather.10.cloned.1.call-start = ((), (), s32[]{:S(2)}) async-start(), calls=%async_computation.13 | async-start | bytes 1474560 | tf_op jit(solution)/shard_map/all_gather | solution.py:43
  285.8 35.7 %all-gather.12.cloned.1.call-start = ((), (), s32[]{:S(2)}) async-start(), calls=%async_computation.16 | async-start | bytes 1474560 | tf_op jit(solution)/shard_map/all_gather | solution.py:43
  286.4 122.8 %reduce-scatter.14.cloned.1.call-start = ((), (), s32[]{:S(2)}) async-start(), calls=%async_computation.14 | async-start | bytes 5898240 | tf_op jit(solution)/shard_map/reduce_scatter | solution.py:63
  313.2 184.1 %reduce-scatter.18.cloned.1.call-start = ((), (), s32[]{:S(2)}) async-start(), calls=%async_computation.17 | async-start | bytes 5898240 | tf_op jit(solution)/shard_map/reduce_scatter | solution.py:63
  332.7 340.6 %reduce-scatter.20.cloned.1.call-start = ((), (), s32[]{:S(2)}) async-start(), calls=%async_computation.18 | async-start | bytes 1474560 | tf_op jit(solution)/shard_map/reduce_scatter | solution.py:81
  500.7 30.7 %collective-permute-start.6 = (f32[256,1152]{1,0:T(8,128)S(1)}, f32[256,1152]{1,0:T(8,128)S(1)}, u32[]{:S(2)}, u32[]{:S(2)}) collective-permute-start(f32[256,1152]{1,0:T(8,128)S(1)} %get-tuple-element.102), channel_id=1, source_target_pairs={{0,4},{4,8},{8,12},{12,0},{1,5},{5,9},{9,13},{13,1},{2,6},{6,10},{... | collective-permute-start | bytes 3538952 | tf_op jit(solution)/shard_map/ppermute | solution.py:21
  502.2 115.3 %copy-start.15 = (f32[288,1152]{1,0:T(8,128)S(1)}, f32[288,1152]{1,0:T(8,128)}, u32[]{:S(2)}) copy-start(f32[288,1152]{1,0:T(8,128)} %param.30) | copy-start | bytes 3981316
  502.2 54.6 %collective-permute-start.3 = (f32[256,1152]{1,0:T(8,128)}, f32[256,1152]{1,0:T(8,128)}, u32[]{:S(2)}, u32[]{:S(2)}) collective-permute-start(f32[256,1152]{1,0:T(8,128)} %get-tuple-element.103), channel_id=1, source_target_pairs={{0,4},{4,8},{8,12},{12,0},{1,5},{5,9},{9,13},{13,1},{2,6},{6,10},{... | collective-permute-start | bytes 3538952 | tf_op jit(solution)/shard_map/ppermute | solution.py:21
  504.2 77.8 %collective-permute-start.8 = (f32[256,1152]{1,0:T(8,128)S(1)}, f32[256,1152]{1,0:T(8,128)S(1)}, u32[]{:S(2)}, u32[]{:S(2)}) collective-permute-start(f32[256,1152]{1,0:T(8,128)S(1)} %get-tuple-element.102), channel_id=1, source_target_pairs={{0,12},{4,0},{8,4},{12,8},{1,13},{5,1},{9,5},{13,9},{2,14},{6,2},{... | collective-permute-start | bytes 3538952 | tf_op jit(solution)/shard_map/ppermute | solution.py:23
  531.5 75.8 %collective-permute-start.7 = (f32[256,1152]{1,0:T(8,128)S(1)}, f32[256,1152]{1,0:T(8,128)S(1)}, u32[]{:S(2)}, u32[]{:S(2)}) collective-permute-start(f32[256,1152]{1,0:T(8,128)S(1)} %collective-permute-done.6), channel_id=1, source_target_pairs={{0,4},{4,8},{8,12},{12,0},{1,5},{5,9},{9,13},{13,1},{2,6},{6,10},{... | collective-permute-start | bytes 3538952 | tf_op jit(solution)/shard_map/ppermute | solution.py:21
  531.5 101.0 %collective-permute-start.5 = (f32[256,1152]{1,0:T(8,128)}, f32[256,1152]{1,0:T(8,128)}, u32[]{:S(2)}, u32[]{:S(2)}) collective-permute-start(f32[256,1152]{1,0:T(8,128)} %get-tuple-element.103), channel_id=1, source_target_pairs={{0,12},{4,0},{8,4},{12,8},{1,13},{5,1},{9,5},{13,9},{2,14},{6,2},{... | collective-permute-start | bytes 3538952 | tf_op jit(solution)/shard_map/ppermute | solution.py:23
  556.8 100.0 %collective-permute-start.4 = (f32[256,1152]{1,0:T(8,128)}, f32[256,1152]{1,0:T(8,128)}, u32[]{:S(2)}, u32[]{:S(2)}) collective-permute-start(f32[256,1152]{1,0:T(8,128)} %collective-permute-done.3), channel_id=1, source_target_pairs={{0,4},{4,8},{8,12},{12,0},{1,5},{5,9},{9,13},{13,1},{2,6},{6,10},{... | collective-permute-start | bytes 3538952 | tf_op jit(solution)/shard_map/ppermute | solution.py:21
  623.6 78.3 %reduce-scatter.16.cloned.1.call-start = ((), (), s32[]{:S(2)}) async-start(), calls=%async_computation.15 | async-start | bytes 1474560 | tf_op jit(solution)/shard_map/reduce_scatter | solution.py:81
  671.0 51.0 %all-gather.14.cloned.1.call-start = ((), (), s32[]{:S(2)}) async-start(), calls=%async_computation.19 | async-start | bytes 1474560 | tf_op jit(solution)/shard_map/all_gather | solution.py:43
  704.4 51.5 %reduce-scatter.22.cloned.1.call-start = ((), (), s32[]{:S(2)}) async-start(), calls=%async_computation.20 | async-start | bytes 1474560 | tf_op jit(solution)/shard_map/reduce_scatter | solution.py:63
  726.4 92.8 %reduce-scatter.24.cloned.1.call-start = ((), (), s32[]{:S(2)}) async-start(), calls=%async_computation.21 | async-start | bytes 2949120 | tf_op jit(solution)/shard_map/reduce_scatter | solution.py:241
  772.8 147.1 %reduce-scatter.26.cloned.1.call-start = ((), (), s32[]{:S(2)}) async-start(), calls=%async_computation.22 | async-start | bytes 1474560 | tf_op jit(solution)/shard_map/reduce_scatter | solution.py:81
  820.3 22.8 %collective-permute-start.9 = (f32[256,864]{0,1:T(8,128)S(1)}, f32[256,864]{0,1:T(8,128)S(1)}, u32[]{:S(2)}, u32[]{:S(2)}) collective-permute-start(f32[256,864]{0,1:T(8,128)S(1)} %bitcast.168), channel_id=1, source_target_pairs={{0,4},{4,8},{8,12},{12,0},{1,5},{5,9},{9,13},{13,1},{2,6},{6,10},{... | collective-permute-start | bytes 2654216 | tf_op jit(solution)/shard_map/ppermute | solution.py:21
  843.2 24.3 %collective-permute-start.10 = (f32[256,864]{0,1:T(8,128)S(1)}, f32[256,864]{0,1:T(8,128)S(1)}, u32[]{:S(2)}, u32[]{:S(2)}) collective-permute-start(f32[256,864]{0,1:T(8,128)S(1)} %collective-permute-done.9), channel_id=1, source_target_pairs={{0,4},{4,8},{8,12},{12,0},{1,5},{5,9},{9,13},{13,1},{2,6},{6,10},{... | collective-permute-start | bytes 2654216 | tf_op jit(solution)/shard_map/ppermute | solution.py:21
  843.2 39.1 %collective-permute-start.11 = (f32[256,864]{0,1:T(8,128)S(1)}, f32[256,864]{0,1:T(8,128)S(1)}, u32[]{:S(2)}, u32[]{:S(2)}) collective-permute-start(f32[256,864]{0,1:T(8,128)S(1)} %bitcast.169), channel_id=1, source_target_pairs={{0,12},{4,0},{8,4},{12,8},{1,13},{5,1},{9,5},{13,9},{2,14},{6,2},{... | collective-permute-start | bytes 2654216 | tf_op jit(solution)/shard_map/ppermute | solution.py:23
  891.0 255.3 %all-reduce.6.cloned.1.call-start = ((), (), s32[]{:S(2)}) async-start(), calls=%async_computation.23 | async-start | bytes 16515072 | tf_op jit(solution)/shard_map/psum | solution.py:273
  (46 other events, 401.0 us)
Sparse Core Ops, SparseCore 0:
  50.4 17.1 all-gather.5
  76.4 66.4 reduce-scatter.9
  145.3 50.1 all-gather.7
  236.7 23.7 reduce-scatter.11
  285.9 16.1 all-gather.9
  304.0 17.4 all-gather.11
  323.8 85.2 reduce-scatter.13
  411.4 85.7 reduce-scatter.17
  623.7 49.5 reduce-scatter.19
  676.3 25.6 reduce-scatter.15
  704.5 17.4 all-gather.13
  726.6 29.3 reduce-scatter.21
  772.9 46.2 reduce-scatter.23
  891.2 25.6 reduce-scatter.25
  952.1 194.1 all-reduce.5
